TPU v7x, 32 devices: a whole 2x2x4 slice. The times are simulated.
32 devices in a mesh: ctx: 8 (over y, x, core), ch: 4 (over z).
Axes of the slice: x: 2, y: 2, z: 4, core: 2. Of those that a mesh axis runs over, the one named last changes fastest.
Arguments:
- query_act: bfloat16 [4096, 4096], P('ctx', 'ch'), may hold values from -6 to 6
- key_act: bfloat16 [4096, 4096], P('ctx', 'ch'), may hold values from -6 to 6
- value_act: bfloat16 [4096, 4096], P('ctx', 'ch'), may hold values from -6 to 6
- filters: bfloat16 [4096, 128], P('ch'), may hold values from -0.5 to 0.5
- proj_weight: bfloat16 [8192, 4096], P('ctx', 'ch'), may hold values from -0.09375 to 0.09375
- cotangent: bfloat16 [4096, 8192], P('ctx', 'ch'), may hold values from -6 to 6
Outputs:
- grad_query: bfloat16 [4096, 4096], P('ctx', 'ch')
- grad_key: bfloat16 [4096, 4096], P('ctx', 'ch')
- grad_value: bfloat16 [4096, 4096], P('ctx', 'ch')
- grad_filter: float32 [4096, 128], P('ch')
- grad_proj: float32 [8192, 4096], P('ctx', 'ch')
All inputs are finite; a program needn't handle non-finite values.
Results may differ from a plain program's by a relative error of at most 0.0051.
Values may be sent and summed in bfloat16 or wider, within the bound.
A program may use at most 192 MiB of HBM per device.

v0:
```python
import jax
import jax.numpy as jnp
import numpy as np
from jax import lax
from jax.sharding import PartitionSpec as P

TAPS = 128


def from_behind(x, axis, by):
    length = lax.axis_size(axis)
    pairs = [(i, i + by) for i in range(length) if 0 <= i + by < length]
    return lax.ppermute(x, axis, pairs)


def basis(points):
    freqs = points // 2
    phase = (2 * np.arange(freqs)[:, None] + 1) * np.arange(points)[None, :] % (2 * points)
    angle = np.pi * phase / points
    return np.concatenate([np.cos(angle), np.sin(angle)], 0).astype(np.float32)


def split(a):
    a = jnp.asarray(a, jnp.float32)
    hi = a.astype(jnp.bfloat16)
    return (hi, (a - hi.astype(jnp.float32)).astype(jnp.bfloat16))


def dot32(a, b):
    return jnp.dot(a, b, preferred_element_type=jnp.float32)


def forward(table, x):
    hi, lo = split(table)
    return dot32(hi, x) + dot32(lo, x)


def backward(table, y):
    thi, tlo = split(table)
    yhi, ylo = split(y)
    return dot32(thi, yhi) + dot32(thi, ylo) + dot32(tlo, yhi)


def halves(x):
    n = x.shape[0] // 2
    return (x[:n], x[n:])


def times(x, f):
    (xc, xs), (fc, fs) = (halves(x), halves(f))
    return jnp.concatenate([xc * fc - xs * fs, xc * fs + xs * fc], 0)


def times_conj(x, f):
    (xc, xs), (fc, fs) = (halves(x), halves(f))
    return jnp.concatenate([xc * fc + xs * fs, xs * fc - xc * fs], 0)


def shards(query_act, key_act, value_act, filters, proj_weight, cotangent):
    tokens = query_act.shape[0]
    points = tokens + TAPS
    table = basis(points)
    inverse = (table.T / (points // 2)).astype(np.float32)
    gathered = lax.all_gather(cotangent, "ch", axis=1, tiled=True)
    weight = lax.all_gather(proj_weight, "ctx", axis=0, tiled=True)
    query_f = query_act.astype(jnp.float32)
    key_f = key_act.astype(jnp.float32)
    value_f = value_act.astype(jnp.float32)
    product = (key_f * value_f).astype(jnp.bfloat16)
    before = from_behind(product[tokens - TAPS :], "ctx", 1)
    filt_spec = forward(table[:, :TAPS], filters.T)
    prod_spec = forward(table[:, :TAPS], before) + forward(table[:, TAPS:], product)
    mixed = backward(inverse[TAPS:], times(prod_spec, filt_spec))
    gated = (query_f * mixed).astype(jnp.bfloat16)
    partial_grad = lax.dot_general(
        gathered, gated, (((0,), (0,)), ((), ())), preferred_element_type=jnp.float32
    ).astype(jnp.bfloat16)
    grad_proj = lax.psum_scatter(partial_grad, "ctx", scatter_dimension=0, tiled=True).astype(
        jnp.float32
    )
    grad_mix = dot32(gathered, weight)
    grad_query = (grad_mix * mixed).astype(jnp.bfloat16)
    grad_gate = (grad_mix * query_f).astype(jnp.bfloat16)
    after = from_behind(grad_gate[:TAPS], "ctx", -1)
    own_spec = forward(table[:, :tokens], grad_gate)
    gate_spec = own_spec + forward(table[:, tokens:], after)
    lags = inverse[TAPS - np.arange(TAPS)]
    local_filter = backward(lags, times_conj(prod_spec, own_spec))
    grad_filter = lax.psum(local_filter, "ctx").T
    grad_prod = backward(inverse[:tokens], times_conj(gate_spec, filt_spec))
    grad_key = (grad_prod * value_f).astype(jnp.bfloat16)
    grad_value = (grad_prod * key_f).astype(jnp.bfloat16)
    return (grad_query, grad_key, grad_value, grad_filter, grad_proj)


def solution(mesh):
    return jax.shard_map(
        shards,
        mesh=mesh,
        in_specs=(
            P("ctx", "ch"),
            P("ctx", "ch"),
            P("ctx", "ch"),
            P("ch", None),
            P("ctx", "ch"),
            P("ctx", "ch"),
        ),
        out_specs=(P("ctx", "ch"), P("ctx", "ch"), P("ctx", "ch"), P("ch", None), P("ctx", "ch")),
        check_vma=False,
    )
```

profile of v0, /device:TPU:0, one launch (start us, length us, event | category | flops | bytes accessed | tf_op | source)
XLA Modules:
  0.0 497.0 jit_solution(8108205557831197759)
XLA Ops:
  8.8 1.3 copy.19
  10.1 1.3 copy.20
  12.4 149.5 %all-gather.3.cloned.1.call-done = bf16[512,8192]{1,0:T(8,128)(2,1)} async-done(((bf16[512,2048]{1,0:T(8,128)(2,1)}), bf16[512,8192]{1,0:T(8,128)(2,1)}) %all-gather.3.cloned.1.call-update) | async-done | bytes 8388624 | tf_op jit(solution)/shard_map/all_gather | solution.py:64
  162.0 90.0 %all-gather.5.cloned.1.call-done = bf16[8192,1024]{1,0:T(8,128)(2,1)} async-done(((bf16[1024,1024]{1,0:T(8,128)(2,1)}), bf16[8192,1024]{1,0:T(8,128)(2,1)}) %all-gather.5.cloned.1.call-update) | async-done | bytes 16777232 | tf_op jit(solution)/shard_map/all_gather | solution.py:65
  251.9 14.9 %fusion.6 = (bf16[512,1024]{1,0:T(8,128)(2,1)S(1)}, f32[512,1024]{1,0:T(8,128)S(1)}) fusion(bf16[512,1024]{1,0:T(8,128)(2,1)} %param.14, bf16[512,8192]{1,0:T(8,128)(2,1)} %all-gather.3.cloned.1.call-done, bf16[8192,1024]{1,0:T(8,128)(2,1)} %all-gather.5.cloned.1.call-done), kind=kOutput, calls=%fused_computation.20 | convolution fusion | flops 8591507456 | bytes 29360128 | tf_op jit(solution)/shard_map/dot_general | solution.py:30
  266.9 1.4 collective-permute-start.1
  272.6 1.0 fusion.8
  273.7 1.0 fusion.21
  275.4 2.7 fusion.3
  278.1 6.7 %collective-permute-start = (bf16[128,1024]{0,1:T(8,128)(2,1)S(1)}, bf16[128,1024]{0,1:T(8,128)(2,1)S(1)}, u32[]{:S(2)}, u32[]{:S(2)}) collective-permute-start(bf16[128,1024]{0,1:T(8,128)(2,1)S(1)} %slice.44), channel_id=1, source_target_pairs={{0,4},{4,8},{8,12},{12,16},{16,20},{20,24},{24,28},{1,5},{5,9},{9,... | collective-permute-start | bytes 786440 | tf_op jit(solution)/shard_map/ppermute | solution.py:13
  285.7 0.9 fusion.37
  288.2 2.5 multiply_add_fusion
  290.7 1.0 fusion.14
  291.8 1.0 fusion.17
  292.8 2.1 multiply_convert_fusion
  294.9 15.9 %convert_bitcast_fusion = bf16[8192,1024]{0,1:T(8,128)(2,1)} fusion(bf16[512,8192]{1,0:T(8,128)(2,1)} %all-gather.3.cloned.1.call-done, f32[512,1024]{1,0:T(8,128)S(1)} %get-tuple-element.24, bf16[512,1024]{1,0:T(8,128)(2,1)S(1)} %copy-done.25), kind=kOutput, calls=%fused_computation | convolution fusion | flops 8599896064 | bytes 28311552 | tf_op jit(solution)/shard_map/dot_general | solution.py:75
  311.0 1.0 copy-done.2
  313.9 1.4 fusion.12
  315.4 2.4 copy.26
  317.7 1.3 copy.25
  319.0 111.5 %reduce-scatter.2.cloned.1.call-done = bf16[1024,1024]{0,1:T(8,128)(2,1)} async-done(((bf16[8192,1024]{0,1:T(8,128)(2,1)}), bf16[1024,1024]{0,1:T(8,128)(2,1)}) %reduce-scatter.2.cloned.1.call-update) | async-done | bytes 2097168 | tf_op jit(solution)/shard_map/reduce_scatter | solution.py:78
  430.5 4.2 copy.27
  434.6 53.9 %all-reduce.2.cloned.1.call-done = f32[1024,128]{1,0:T(8,128)} async-done(((f32[1024,128]{1,0:T(8,128)}), f32[1024,128]{1,0:T(8,128)}) %all-reduce.2.cloned.1.call-update) | async-done | bytes 524304 | tf_op jit(solution)/shard_map/psum | solution.py:89
  488.6 1.9 copy.33
  (75 shorter events, 12.2 us)
Async XLA Ops:
  7.2 4.2 copy-start
  7.2 1.6 copy-start.10
  7.2 154.8 %all-gather.3.cloned.1.call-start = ((), (), s32[]{:S(2)}) async-start(), calls=%async_computation.1 | async-start | bytes 10485760 | tf_op jit(solution)/shard_map/all_gather | solution.py:64
  7.9 2.2 copy-start.11
  7.9 244.0 %all-gather.5.cloned.1.call-start = ((), (), s32[]{:S(2)}) async-start(), calls=%async_computation.2 | async-start | bytes 18874368 | tf_op jit(solution)/shard_map/all_gather | solution.py:65
  8.7 2.7 copy-start.20
  8.7 421.8 %reduce-scatter.2.cloned.1.call-start = ((), (), s32[]{:S(2)}) async-start(), calls=%async_computation.4 | async-start | bytes 18874368 | tf_op jit(solution)/shard_map/reduce_scatter | solution.py:78
  10.1 1.8 copy-start.13
  12.4 255.9 %copy-start.9 = (bf16[640,512]{1,0:T(8,128)(2,1)S(1)}, bf16[640,512]{1,0:T(8,128)(2,1)}, u32[]{:S(2)}) copy-start(bf16[640,512]{1,0:T(8,128)(2,1)} %constant.33) | copy-start | bytes 1966084
  266.9 2.3 copy-start.18
  266.9 3.6 collective-permute-start.1
  273.7 1.5 copy-start.6
  273.7 1.7 copy-start.12
  275.4 9.4 %copy-start.17 = (bf16[640,512]{1,0:T(8,128)(2,1)S(1)}, bf16[640,512]{1,0:T(8,128)(2,1)}, u32[]{:S(2)}) copy-start(bf16[640,512]{1,0:T(8,128)(2,1)} %constant.28) | copy-start | bytes 1966084
  278.1 7.6 %copy-start.16 = (bf16[640,512]{1,0:T(8,128)(2,1)S(1)}, bf16[640,512]{1,0:T(8,128)(2,1)}, u32[]{:S(2)}) copy-start(bf16[640,512]{1,0:T(8,128)(2,1)} %constant.25) | copy-start | bytes 1966084
  278.1 8.5 %collective-permute-start = (bf16[128,1024]{0,1:T(8,128)(2,1)S(1)}, bf16[128,1024]{0,1:T(8,128)(2,1)S(1)}, u32[]{:S(2)}, u32[]{:S(2)}) collective-permute-start(bf16[128,1024]{0,1:T(8,128)(2,1)S(1)} %slice.44), channel_id=1, source_target_pairs={{0,4},{4,8},{8,12},{12,16},{16,20},{20,24},{24,28},{1,5},{5,9},{9,... | collective-permute-start | bytes 786440 | tf_op jit(solution)/shard_map/ppermute | solution.py:13
  288.2 2.5 copy-start.15
  292.7 2.1 copy-start.25
  310.7 1.3 copy-start.2
  310.7 1.7 copy-start.3
  310.7 1.7 copy-start.19
  310.8 177.8 %all-reduce.2.cloned.1.call-start = ((), (), s32[]{:S(2)}) async-start(), calls=%async_computation.3 | async-start | bytes 1048576 | tf_op jit(solution)/shard_map/psum | solution.py:89
  315.3 2.4 copy-start.4
  430.5 60.0 %copy-start.1 = (bf16[1024,128]{1,0:T(8,128)(2,1)S(1)}, bf16[1024,128]{1,0:T(8,128)(2,1)}, u32[]{:S(2)}) copy-start(bf16[1024,128]{1,0:T(8,128)(2,1)} %param.17) | copy-start | bytes 786436
  (8 other events, 8.3 us)
Sparse Core Ops, SparseCore 0:
  9.6 152.3 all-gather.2
  163.9 88.0 all-gather.4
  310.9 119.5 reduce-scatter.1
  434.0 54.5 all-reduce.1
where the time goes:
time: 498 us; the launch traced here: 497 us
  waiting for transfers between devices  407 us (82%)
  matrix products  48.7 us (10%)
  local copies, waits for them, and re-layouts  15.9 us (3%)
  between operations  14.1 us (3%)
  starting transfers between devices  8.5 us (2%)
    all_gather x1, waiting for transfers between devices, shards(): gathered = lax.all_gather(cotangent, 'ch', axis=1, tiled=True)  150 us
    reduce_scatter x1, waiting for transfers between devices, shards(): lax.psum_scatter(partial_grad, 'ctx', scatter_dimension=0, tiled=True)  111 us
    all_gather x1, waiting for transfers between devices, shards(): weight = lax.all_gather(proj_weight, 'ctx', axis=0, tiled=True)  90 us
    psum x1, waiting for transfers between devices, shards(): grad_filter = lax.psum(local_filter, 'ctx').T  53.9 us
    dot_general x20, matrix products, dot32(): return jnp.dot(a, b, preferred_element_type=jnp.float32)  32.9 us
    dot_general x1, matrix products, shards(): lax.dot_general(gathered, gated, (((0,), (0,)), ((), ())), preferred_elem...  15.9 us
    unnamed x58, local copies, waits for them, and re-layouts  15.9 us
  transfers between devices with their start and end apart: 6, of which 5 were waited for; matrix products, arithmetic and copies ran while one was open for 4% of the time, Pallas kernels for 0%

commit v1 on v0

--- a/solution.py
+++ b/solution.py
@@ -5,6 +5,28 @@
 from jax.sharding import PartitionSpec as P
 
 TAPS = 128
+
+
+def joined_along(parts, dim):
+    shape = list(parts.shape[1:])
+    shape[dim] *= parts.shape[0]
+    return jnp.moveaxis(parts, 0, dim).reshape(shape)
+
+
+def gather_around(shard, axis, dim):
+    size = lax.axis_size(axis)
+    pairs = [(i, (i + 1) % size) for i in range(size)]
+    back = [(b, a) for a, b in pairs]
+    lower, upper = ([], [])
+    for hop in range(size - 1):
+        if hop % 2 == 0:
+            lower.append(lax.ppermute(lower[-1] if lower else shard, axis, pairs))
+        else:
+            upper.append(lax.ppermute(upper[-1] if upper else shard, axis, back))
+    blocks = jnp.stack([*lower[::-1], shard, *upper])
+    shift = lax.axis_index(axis) - len(lower)
+    blocks = blocks[(jnp.arange(size) - shift) % size]
+    return joined_along(blocks, dim)
 
 
 def from_behind(x, axis, by):
@@ -62,7 +84,7 @@
     table = basis(points)
     inverse = (table.T / (points // 2)).astype(np.float32)
     gathered = lax.all_gather(cotangent, "ch", axis=1, tiled=True)
-    weight = lax.all_gather(proj_weight, "ctx", axis=0, tiled=True)
+    weight = gather_around(proj_weight, "ctx", 0)
     query_f = query_act.astype(jnp.float32)
     key_f = key_act.astype(jnp.float32)
     value_f = value_act.astype(jnp.float32)

time: 498 us -> 470 us (0.944)
  waiting for transfers between devices: 407 us -> 325 us
  local copies, waits for them, and re-layouts: 15.9 us -> 53.8 us
  other arithmetic: 3.06 us -> 16.7 us
    ppermute x0 -> x7, waiting for transfers between devices: none -> 153 us  [the longest x4 153 us: gather_around(): lower.append(lax.ppermute(lower[-1] if lower else shard, axis, pairs))]
    all_gather x1, waiting for transfers between devices: 150 us -> 0.01 us  [shards(): gathered = lax.all_gather(cotangent, 'ch', axis=1, tiled=True)]
    all_gather x1 -> x0, waiting for transfers between devices: 90 us -> none  [shards(): weight = lax.all_gather(proj_weight, 'ctx', axis=0, tiled=True)]
    gather x0 -> x3, local copies, waits for them, and re-layouts: none -> 22.4 us  [gather_around(): blocks = blocks[(jnp.arange(size) - shift) % size]]
    unnamed x58 -> x75, local copies, waits for them, and re-layouts: 15.9 us -> 31.1 us
    unnamed x0 -> x1, other arithmetic: none -> 13.7 us
    ppermute x0 -> x7, starting transfers between devices: none -> 7.24 us  [the longest x3 6.73 us: gather_around(): upper.append(lax.ppermute(upper[-1] if upper else shard, axis, back))]
  transfers between devices with their start and end apart: 6 -> 12, of which waited for: 5 -> 7; matrix products, arithmetic and copies ran while one was open for 4% -> 14% of each run, Pallas kernels for 0% -> 0%
where the time goes in v1:
time: 470 us; the launch traced here: 469 us
  waiting for transfers between devices  325 us (69%)
  local copies, waits for them, and re-layouts  53.8 us (11%)
  matrix products  48.5 us (10%)
  other arithmetic  16.7 us (4%)
  between operations  14.2 us (3%)
  starting transfers between devices  11.5 us (2%)
    ppermute x4, waiting for transfers between devices, gather_around(): lower.append(lax.ppermute(lower[-1] if lower else shard, axis, pairs))  153 us
    reduce_scatter x1, waiting for transfers between devices, shards(): lax.psum_scatter(partial_grad, 'ctx', scatter_dimension=0, tiled=True)  116 us
    psum x1, waiting for transfers between devices, shards(): grad_filter = lax.psum(local_filter, 'ctx').T  54.1 us
    dot_general x20, matrix products, dot32(): return jnp.dot(a, b, preferred_element_type=jnp.float32)  33.4 us
    unnamed x75, local copies, waits for them, and re-layouts  31.1 us
    gather x3, local copies, waits for them, and re-layouts, gather_around(): blocks = blocks[(jnp.arange(size) - shift) % size]  22.4 us
    dot_general x1, matrix products, shards(): lax.dot_general(gathered, gated, (((0,), (0,)), ((), ())), preferred_elem...  15.1 us
    unnamed x1, other arithmetic  13.7 us
  transfers between devices with their start and end apart: 12, of which 7 were waited for; matrix products, arithmetic and copies ran while one was open for 14% of the time, Pallas kernels for 0%

profile of v1, /device:TPU:0, one launch (start us, length us, event | category | flops | bytes accessed | tf_op | source)
XLA Modules:
  0.0 469.4 jit_solution(17967071979211600506)
XLA Ops:
  8.0 26.7 %collective-permute-done = bf16[1024,1024]{1,0:T(8,128)(2,1)} collective-permute-done((bf16[1024,1024]{1,0:T(8,128)(2,1)}, bf16[1024,1024]{1,0:T(8,128)(2,1)}, u32[]{:S(2)}, u32[]{:S(2)}) %collective-permute-start) | collective-permute-done | bytes 2097184 | tf_op jit(solution)/shard_map/ppermute | solution.py:23
  34.7 2.6 collective-permute-start.4
  37.3 44.8 %collective-permute-done.1 = bf16[1024,1024]{1,0:T(8,128)(2,1)S(1)} collective-permute-done((bf16[1024,1024]{1,0:T(8,128)(2,1)}, bf16[1024,1024]{1,0:T(8,128)(2,1)S(1)}, u32[]{:S(2)}, u32[]{:S(2)}) %collective-permute-start.1) | collective-permute-done | bytes 2097184 | tf_op jit(solution)/shard_map/ppermute | solution.py:23
  84.9 44.9 %collective-permute-done.2 = bf16[1024,1024]{1,0:T(8,128)(2,1)} collective-permute-done((bf16[1024,1024]{1,0:T(8,128)(2,1)S(1)}, bf16[1024,1024]{1,0:T(8,128)(2,1)}, u32[]{:S(2)}, u32[]{:S(2)}) %collective-permute-start.2) | collective-permute-done | bytes 2097184 | tf_op jit(solution)/shard_map/ppermute | solution.py:23
  129.8 2.4 copy.22
  135.9 2.7 collective-permute-start.6
  138.6 36.9 %collective-permute-done.3 = bf16[1024,1024]{1,0:T(8,128)(2,1)} collective-permute-done((bf16[1024,1024]{1,0:T(8,128)(2,1)}, bf16[1024,1024]{1,0:T(8,128)(2,1)}, u32[]{:S(2)}, u32[]{:S(2)}) %collective-permute-start.3) | collective-permute-done | bytes 2097184 | tf_op jit(solution)/shard_map/ppermute | solution.py:23
  177.3 1.9 bitcast_dynamic-update-slice_fusion.6
  179.7 1.9 bitcast_dynamic-update-slice_fusion.4
  185.8 6.3 %fusion.39 = (bf16[8,512,1024]{2,1,0:T(8,128)(2,1)}, bf16[8,512,1024]{2,1,0:T(8,128)(2,1)}) fusion(bf16[8,1024,1024]{2,1,0:T(8,128)(2,1)S(1)} %bitcast_dynamic-update-slice_fusion), kind=kLoop, calls=%fused_computation.71 | loop fusion | bytes 33554432 | tf_op jit(solution)/shard_map/gather | solution.py:28
  192.1 8.1 %gather_fusion = bf16[8,512,1024]{2,1,0:T(8,128)(2,1)} fusion(bf16[8,512,1024]{2,1,0:T(8,128)(2,1)} %get-tuple-element.10, s32[1024]{0:T(1024)S(1)} %pad_clamp_fusion), kind=kCustom, calls=%fused_computation | custom fusion | bytes 16777248 | tf_op jit(solution)/shard_map/gather | solution.py:28
  200.2 8.1 %gather_fusion.1 = bf16[8,512,1024]{2,1,0:T(8,128)(2,1)} fusion(bf16[8,512,1024]{2,1,0:T(8,128)(2,1)} %get-tuple-element.11, s32[1024]{0:T(1024)S(1)} %pad_clamp_fusion), kind=kCustom, calls=%fused_computation.1 | custom fusion | bytes 16777248 | tf_op jit(solution)/shard_map/gather | solution.py:28
  208.3 13.7 %pad_maximum_fusion = bf16[8,1024,1024]{2,1,0:T(8,128)(2,1)} fusion(bf16[8,512,1024]{2,1,0:T(8,128)(2,1)} %gather_fusion.1, bf16[8,512,1024]{2,1,0:T(8,128)(2,1)} %gather_fusion), kind=kLoop, calls=%fused_computation.2 | loop fusion | flops 33554432 | bytes 33554432
  221.9 15.1 %fusion.6 = (bf16[512,1024]{0,1:T(8,128)(2,1)S(1)}, f32[1024,512]{1,0:T(8,128)S(1)}) fusion(bf16[512,1024]{0,1:T(8,128)(2,1)} %copy.22, bf16[8192,1024]{1,0:T(8,128)(2,1)} %bitcast.66, bf16[512,8192]{1,0:T(8,128)(2,1)} %all-gather.2.cloned.1.call-done), kind=kOutput, calls=%fused_computation.23 | convolution fusion | flops 8591507456 | bytes 29360128 | tf_op jit(solution)/shard_map/dot_general | solution.py:52
  246.5 2.7 fusion.3
  249.3 2.6 collective-permute-start.7
  255.3 2.4 multiply_add_fusion
  259.8 2.1 fusion.8
  262.0 15.1 %convert_bitcast_fusion = bf16[8192,1024]{0,1:T(8,128)(2,1)} fusion(bf16[512,8192]{1,0:T(8,128)(2,1)} %all-gather.2.cloned.1.call-done, f32[512,1024]{0,1:T(8,128)S(1)} %get-tuple-element.26, bf16[512,1024]{0,1:T(8,128)(2,1)S(1)} %copy-done.16), kind=kOutput, calls=%fused_computation.3 | convolution fusion | flops 8599896064 | bytes 28311552 | tf_op jit(solution)/shard_map/dot_general | solution.py:97
  281.7 2.4 copy.26
  286.7 116.1 %reduce-scatter.2.cloned.1.call-done = bf16[1024,1024]{0,1:T(8,128)(2,1)} async-done(((bf16[8192,1024]{0,1:T(8,128)(2,1)}), bf16[1024,1024]{0,1:T(8,128)(2,1)}) %reduce-scatter.2.cloned.1.call-update) | async-done | bytes 2097168 | tf_op jit(solution)/shard_map/reduce_scatter | solution.py:100
  402.8 4.2 copy.28
  406.9 54.1 %all-reduce.2.cloned.1.call-done = f32[1024,128]{1,0:T(8,128)} async-done(((f32[1024,128]{1,0:T(8,128)}), f32[1024,128]{1,0:T(8,128)}) %all-reduce.2.cloned.1.call-update) | async-done | bytes 524304 | tf_op jit(solution)/shard_map/psum | solution.py:111
  461.0 1.9 copy.40
  (110 shorter events, 35.6 us)
Async XLA Ops:
  7.2 127.7 %copy-start = (bf16[1024,128]{1,0:T(8,128)(2,1)S(1)}, bf16[1024,128]{1,0:T(8,128)(2,1)}, u32[]{:S(2)}) copy-start(bf16[1024,128]{1,0:T(8,128)(2,1)} %param.17) | copy-start | bytes 786436
  7.2 27.5 %copy-start.10 = (bf16[1024,1024]{1,0:T(8,128)(2,1)S(1)}, bf16[1024,1024]{1,0:T(8,128)(2,1)}, u32[]{:S(2)}) copy-start(bf16[1024,1024]{1,0:T(8,128)(2,1)} %param.18) | copy-start | bytes 6291460
  7.2 125.0 %copy-start.14 = (bf16[512,1024]{1,0:T(8,128)(2,1)S(1)}, bf16[512,1024]{1,0:T(8,128)(2,1)}, u32[]{:S(2)}) copy-start(bf16[512,1024]{1,0:T(8,128)(2,1)} %param.15) | copy-start | bytes 3145732
  7.2 214.7 %all-gather.2.cloned.1.call-start = ((), (), s32[]{:S(2)}) async-start(), calls=%async_computation.1 | async-start | bytes 10485760 | tf_op jit(solution)/shard_map/all_gather | solution.py:86
  7.2 27.4 %collective-permute-start = (bf16[1024,1024]{1,0:T(8,128)(2,1)}, bf16[1024,1024]{1,0:T(8,128)(2,1)}, u32[]{:S(2)}, u32[]{:S(2)}) collective-permute-start(bf16[1024,1024]{1,0:T(8,128)(2,1)} %param.18), channel_id=1, source_target_pairs={{0,4},{4,8},{8,12},{12,16},{16,20},{20,24},{24,28},{28,0},{1,5},{5... | collective-permute-start | bytes 6291464 | tf_op jit(solution)/shard_map/ppermute | solution.py:23
  7.9 394.9 %reduce-scatter.2.cloned.1.call-start = ((), (), s32[]{:S(2)}) async-start(), calls=%async_computation.3 | async-start | bytes 18874368 | tf_op jit(solution)/shard_map/reduce_scatter | solution.py:100
  34.7 47.5 %collective-permute-start.1 = (bf16[1024,1024]{1,0:T(8,128)(2,1)}, bf16[1024,1024]{1,0:T(8,128)(2,1)S(1)}, u32[]{:S(2)}, u32[]{:S(2)}) collective-permute-start(bf16[1024,1024]{1,0:T(8,128)(2,1)} %collective-permute-done), channel_id=1, source_target_pairs={{0,4},{4,8},{8,12},{12,16},{16,20},{20,24},{24,28},{28,0},{1,5},{5... | collective-permute-start | bytes 6291464 | tf_op jit(solution)/shard_map/ppermute | solution.py:23
  34.7 47.5 %collective-permute-start.4 = (bf16[1024,1024]{1,0:T(8,128)(2,1)S(1)}, bf16[1024,1024]{1,0:T(8,128)(2,1)}, u32[]{:S(2)}, u32[]{:S(2)}) collective-permute-start(bf16[1024,1024]{1,0:T(8,128)(2,1)S(1)} %copy-done.10), channel_id=1, source_target_pairs={{4,0},{8,4},{12,8},{16,12},{20,16},{24,20},{28,24},{0,28},{5,1},{9... | collective-permute-start | bytes 6291464 | tf_op jit(solution)/shard_map/ppermute | solution.py:25
  82.2 47.6 %collective-permute-start.2 = (bf16[1024,1024]{1,0:T(8,128)(2,1)S(1)}, bf16[1024,1024]{1,0:T(8,128)(2,1)}, u32[]{:S(2)}, u32[]{:S(2)}) collective-permute-start(bf16[1024,1024]{1,0:T(8,128)(2,1)S(1)} %collective-permute-done.1), channel_id=1, source_target_pairs={{0,4},{4,8},{8,12},{12,16},{16,20},{20,24},{24,28},{28,0},{1,5},{5... | collective-permute-start | bytes 6291464 | tf_op jit(solution)/shard_map/ppermute | solution.py:23
  83.5 52.4 %collective-permute-start.5 = (bf16[1024,1024]{1,0:T(8,128)(2,1)}, bf16[1024,1024]{1,0:T(8,128)(2,1)}, u32[]{:S(2)}, u32[]{:S(2)}) collective-permute-start(bf16[1024,1024]{1,0:T(8,128)(2,1)} %collective-permute-done.4), channel_id=1, source_target_pairs={{4,0},{8,4},{12,8},{16,12},{20,16},{24,20},{28,24},{0,28},{5,1},{9... | collective-permute-start | bytes 6291464 | tf_op jit(solution)/shard_map/ppermute | solution.py:25
  129.8 45.7 %collective-permute-start.3 = (bf16[1024,1024]{1,0:T(8,128)(2,1)}, bf16[1024,1024]{1,0:T(8,128)(2,1)}, u32[]{:S(2)}, u32[]{:S(2)}) collective-permute-start(bf16[1024,1024]{1,0:T(8,128)(2,1)} %collective-permute-done.2), channel_id=1, source_target_pairs={{0,4},{4,8},{8,12},{12,16},{16,20},{20,24},{24,28},{28,0},{1,5},{5... | collective-permute-start | bytes 6291464 | tf_op jit(solution)/shard_map/ppermute | solution.py:23
  129.8 3.7 copy-start.15
  132.2 2.7 copy-start.25
  135.9 49.7 %collective-permute-start.6 = (bf16[1024,1024]{1,0:T(8,128)(2,1)}, bf16[1024,1024]{1,0:T(8,128)(2,1)S(1)}, u32[]{:S(2)}, u32[]{:S(2)}) collective-permute-start(bf16[1024,1024]{1,0:T(8,128)(2,1)} %collective-permute-done.5), channel_id=1, source_target_pairs={{4,0},{8,4},{12,8},{16,12},{20,16},{24,20},{28,24},{0,28},{5,1},{9... | collective-permute-start | bytes 6291464 | tf_op jit(solution)/shard_map/ppermute | solution.py:25
  221.9 15.2 %copy-start.23 = (bf16[640,512]{1,0:T(8,128)(2,1)S(1)}, bf16[640,512]{1,0:T(8,128)(2,1)}, u32[]{:S(2)}) copy-start(bf16[640,512]{1,0:T(8,128)(2,1)} %constant.59) | copy-start | bytes 1966084
  237.1 2.5 copy-start.22
  238.0 3.6 copy-start.27
  238.0 3.6 collective-permute-start.8
  246.5 5.4 %copy-start.21 = (bf16[640,512]{1,0:T(8,128)(2,1)S(1)}, bf16[640,512]{1,0:T(8,128)(2,1)}, u32[]{:S(2)}) copy-start(bf16[640,512]{1,0:T(8,128)(2,1)} %constant.51) | copy-start | bytes 1966084
  249.3 3.5 copy-start.20
  249.3 4.4 collective-permute-start.7
  277.1 184.0 %all-reduce.2.cloned.1.call-start = ((), (), s32[]{:S(2)}) async-start(), calls=%async_computation.2 | async-start | bytes 1048576 | tf_op jit(solution)/shard_map/psum | solution.py:111
  281.7 3.7 copy-start.7
  402.8 60.1 %copy-start.1 = (bf16[1024,128]{1,0:T(8,128)(2,1)S(1)}, bf16[1024,128]{1,0:T(8,128)(2,1)}, u32[]{:S(2)}) copy-start(bf16[1024,128]{1,0:T(8,128)(2,1)} %param.17) | copy-start | bytes 786436
  (18 other events, 29.4 us)
Sparse Core Ops, SparseCore 0:
  9.6 152.3 all-gather.1
  277.2 125.5 reduce-scatter.1
  406.5 54.5 all-reduce.1
